TPU v7x, 1024 devices: a whole 8x8x8 slice. The times are simulated.
1024 devices in a mesh: vel: 64 (over z_hi, x, core), space: 16 (over y, z_lo).
Axes of the slice: x: 8, y: 8, z: 8 (z_hi: 4, z_lo: 2; z = z_hi * 2 + z_lo), core: 2. Of those that a mesh axis runs over, the one named last changes fastest.
Arguments:
- distribution: float32 [1024, 256, 512], P('vel', 'space'), may hold values from -6 to 6
- courant: float32 [1024], replicated, may hold values from -0.9 to 0.9
- gain_matrix: bfloat16 [1024, 1024], replicated, may hold values from -0.1875 to 0.1875
- product_matrix: bfloat16 [1024, 1024], replicated, may hold values from -0.1875 to 0.1875
- collision_rate: float32 [256, 512], P('space'), may hold values from 0.5 to 2
Outputs:
- final_state: float32 [1024, 256, 512], P('vel', 'space')
All inputs are finite; a program needn't handle non-finite values.
Results may differ from a plain program's by a relative error of at most 0.0016.
Values may be sent and summed in bfloat16 or wider, within the bound.
A program may use at most 64 MiB of HBM per device.

v0:
```python
import jax
import jax.numpy as jnp
from jax import lax
from jax.sharding import PartitionSpec as P

STEPS = 2


time_step = 0.2


def with_halo(block, sides, width):
    for axis, dim in sides:
        count = lax.axis_size(axis)
        forward = [(i, i + 1) for i in range(count - 1)]
        forward.append((count - 1, 0))
        backward = [(target, source) for source, target in forward]
        low = lax.ppermute(
            lax.slice_in_dim(block, block.shape[dim] - width, None, axis=dim), axis, forward
        )
        high = lax.ppermute(lax.slice_in_dim(block, 0, width, axis=dim), axis, backward)
        block = jnp.concatenate([low, block, high], axis=dim)
    return block


def minmod(first, second):
    return jnp.maximum(jnp.minimum(first, second), 0.0) + jnp.minimum(
        jnp.maximum(first, second), 0.0
    )


def change(widened, speeds):
    differ = widened[:, 1:] - widened[:, :-1]
    slopes = minmod(differ[:, 1:], differ[:, :-1])
    inner = widened.shape[1] - 4
    left_value = widened[:, 1 : inner + 2]
    right_value = widened[:, 2 : inner + 3]
    left_slope = slopes[:, 0 : inner + 1]
    right_slope = slopes[:, 1 : inner + 2]
    upward = jnp.maximum(speeds, 0.0)
    downward = jnp.minimum(speeds, 0.0)
    fluxes = upward * (left_value + 0.5 * (1.0 - speeds) * left_slope) + downward * (
        right_value - 0.5 * (1.0 + speeds) * right_slope
    )
    return -(fluxes[:, 1:] - fluxes[:, :-1])


def extend(field):
    return with_halo(field, (("space", 1),), 2)


def advect(field, speeds):
    section = field + change(extend(field), speeds)
    return 0.5 * field + 0.5 * (section + change(extend(section), speeds))


def collide(pieces, gain_matrix, product_matrix):
    columns = pieces.reshape(pieces.shape[0], -1)
    first_term = jnp.dot(gain_matrix, columns, preferred_element_type=jnp.float32)
    second_term = jnp.dot(product_matrix, columns, preferred_element_type=jnp.float32)
    return (first_term * second_term).astype(jnp.bfloat16).reshape(pieces.shape)


def update(smoothed, rounded, gained, rate):
    return smoothed + time_step * (gained.astype(jnp.float32) - rate * rounded.astype(jnp.float32))


def body(distribution, courant, gain_matrix, product_matrix, collision_rate):
    local_count = distribution.shape[0]
    groups = lax.axis_size("vel")
    member = lax.axis_index("vel")
    own_speeds = lax.dynamic_slice_in_dim(courant, member * local_count, local_count, 0)[
        :, None, None
    ]
    field = distribution
    for step_index in range(STEPS):
        smoothed = advect(field, own_speeds)
        rounded = smoothed.astype(jnp.bfloat16)
        grouped = rounded.reshape(local_count, groups, -1)
        gained = lax.all_to_all(
            collide(
                lax.all_to_all(grouped, "vel", split_axis=1, concat_axis=0, tiled=True),
                gain_matrix,
                product_matrix,
            ),
            "vel",
            split_axis=0,
            concat_axis=1,
            tiled=True,
        )
        field = update(smoothed, rounded, gained.reshape(rounded.shape), collision_rate[None])
    return field


def solution(mesh):
    in_specs = (P("vel", "space", None), P(), P(), P(), P("space", None))
    out_specs = P("vel", "space", None)
    return jax.shard_map(body, mesh=mesh, in_specs=in_specs, out_specs=out_specs, check_vma=False)
```

profile of v0, /device:TPU:1, one launch (start us, length us, event | category | flops | bytes accessed | tf_op | source)
XLA Modules:
  0.0 162.2 jit_solution(1685828752279004742)
XLA Ops:
  0.0 1.2 fusion.43
  1.2 5.7 %collective-permute-start = (f32[16,2,512]{2,1,0:T(2,128)S(1)}, f32[16,2,512]{2,1,0:T(2,128)S(1)}, u32[]{:S(2)}, u32[]{:S(2)}) collective-permute-start(f32[16,2,512]{2,1,0:T(2,128)S(1)} %get-tuple-element.17), channel_id=1, source_target_pairs={{0,1},{1,2},{2,3},{3,4},{4,5},{5,6},{6,7},{7,8},{8,9},{9,10},{10,1... | collective-permute-start | bytes 196616 | tf_op jit(solution)/shard_map/ppermute | solution.py:18
  7.0 5.6 %collective-permute-start.1 = (f32[16,2,512]{2,1,0:T(2,128)S(1)}, f32[16,2,512]{2,1,0:T(2,128)S(1)}, u32[]{:S(2)}, u32[]{:S(2)}) collective-permute-start(f32[16,2,512]{2,1,0:T(2,128)S(1)} %get-tuple-element.18), channel_id=1, source_target_pairs={{1,0},{2,1},{3,2},{4,3},{5,4},{6,5},{7,6},{8,7},{9,8},{10,9},{11,1... | collective-permute-start | bytes 196616 | tf_op jit(solution)/shard_map/ppermute | solution.py:21
  12.6 0.8 broadcast_maximum_fusion
  13.4 0.5 collective-permute-done.1
  13.9 1.2 pad_maximum_fusion.8
  15.1 0.1 slice_subtract_fusion.3
  15.2 0.2 minimum_add_fusion.3
  15.4 0.7 copy-done.1
  16.1 0.4 fusion.21
  16.6 0.1 fusion.35
  16.8 1.9 %collective-permute-start.2 = (f32[16,2,512]{2,1,0:T(2,128)S(1)}, f32[16,2,512]{2,1,0:T(2,128)S(1)}, u32[]{:S(2)}, u32[]{:S(2)}) collective-permute-start(f32[16,2,512]{2,1,0:T(2,128)S(1)} %get-tuple-element.15), channel_id=1, source_target_pairs={{0,1},{1,2},{2,3},{3,4},{4,5},{5,6},{6,7},{7,8},{8,9},{9,10},{10,1... | collective-permute-start | bytes 196616 | tf_op jit(solution)/shard_map/ppermute | solution.py:18
  18.7 5.8 %collective-permute-start.3 = (f32[16,2,512]{2,1,0:T(2,128)S(1)}, f32[16,2,512]{2,1,0:T(2,128)S(1)}, u32[]{:S(2)}, u32[]{:S(2)}) collective-permute-start(f32[16,2,512]{2,1,0:T(2,128)S(1)} %get-tuple-element.16), channel_id=1, source_target_pairs={{1,0},{2,1},{3,2},{4,3},{5,4},{6,5},{7,6},{8,7},{9,8},{10,9},{11,1... | collective-permute-start | bytes 196616 | tf_op jit(solution)/shard_map/ppermute | solution.py:21
  24.5 1.3 collective-permute-done.3
  25.8 0.1 pad_maximum_fusion.9
  25.9 0.1 slice_subtract_fusion.2
  26.1 0.2 minimum_add_fusion.2
  26.3 0.4 fusion.16
  26.7 0.2 fusion.38
  26.9 0.2 reshape.43
  27.1 0.2 copy.16
  27.3 36.9 %all_to_all.48 = bf16[16,64,128]{2,0,1:T(8,128)(2,1)S(1)} all-to-all(bf16[16,64,128]{2,0,1:T(8,128)(2,1)S(1)} %copy.16), channel_id=1, replica_groups=mesh['vel'=64,'space'=16] {'vel'}, dimensions={1} | all-to-all | bytes 524288 | tf_op jit(solution)/shard_map/all_to_all | solution.py:82
  64.2 0.8 fusion.44
  65.1 0.8 fusion.3
  65.9 0.6 broadcast.51
  66.5 0.8 reduce
  67.3 0.2 copy.24
  67.5 0.1 reshape.53
  67.6 19.8 %all_to_all.49 = bf16[64,2,1024]{2,1,0:T(2,128)(2,1)} all-to-all(bf16[64,2,1024]{2,1,0:T(2,128)(2,1)S(1)} %reshape.53), channel_id=1, replica_groups=mesh['vel'=64,'space'=16] {'vel'}, dimensions={0} | all-to-all | bytes 524288 | tf_op jit(solution)/shard_map/all_to_all | solution.py:80
  87.4 2.1 %reshape.54 = bf16[1024,1,128]{2,1,0:T(2,128)(2,1)S(1)} reshape(bf16[64,2,1024]{2,1,0:T(2,128)(2,1)} %all_to_all.49) | data formatting | bytes 524288
  89.6 1.0 copy.19
  90.5 1.1 reshape.49
  91.7 0.1 multiply_add_fusion.1
  91.8 0.1 fusion.41
  91.9 2.2 %collective-permute-start.4 = (f32[16,2,512]{2,1,0:T(2,128)S(1)}, f32[16,2,512]{2,1,0:T(2,128)S(1)}, u32[]{:S(2)}, u32[]{:S(2)}) collective-permute-start(f32[16,2,512]{2,1,0:T(2,128)S(1)} %get-tuple-element.13), channel_id=1, source_target_pairs={{0,1},{1,2},{2,3},{3,4},{4,5},{5,6},{6,7},{7,8},{8,9},{9,10},{10,1... | collective-permute-start | bytes 196616 | tf_op jit(solution)/shard_map/ppermute | solution.py:18
  94.1 5.8 %collective-permute-start.5 = (f32[16,2,512]{2,1,0:T(2,128)S(1)}, f32[16,2,512]{2,1,0:T(2,128)S(1)}, u32[]{:S(2)}, u32[]{:S(2)}) collective-permute-start(f32[16,2,512]{2,1,0:T(2,128)S(1)} %get-tuple-element.14), channel_id=1, source_target_pairs={{1,0},{2,1},{3,2},{4,3},{5,4},{6,5},{7,6},{8,7},{9,8},{10,9},{11,1... | collective-permute-start | bytes 196616 | tf_op jit(solution)/shard_map/ppermute | solution.py:21
  99.8 0.4 collective-permute-done.4
  100.2 0.9 collective-permute-done.5
  101.2 0.1 pad_maximum_fusion.10
  101.3 0.1 slice_subtract_fusion.1
  101.4 0.2 minimum_add_fusion.1
  101.6 0.4 fusion.11
  102.0 0.1 fusion.29
  102.2 1.9 %collective-permute-start.6 = (f32[16,2,512]{2,1,0:T(2,128)S(1)}, f32[16,2,512]{2,1,0:T(2,128)S(1)}, u32[]{:S(2)}, u32[]{:S(2)}) collective-permute-start(f32[16,2,512]{2,1,0:T(2,128)S(1)} %get-tuple-element.11), channel_id=1, source_target_pairs={{0,1},{1,2},{2,3},{3,4},{4,5},{5,6},{6,7},{7,8},{8,9},{9,10},{10,1... | collective-permute-start | bytes 196616 | tf_op jit(solution)/shard_map/ppermute | solution.py:18
  104.2 6.2 %collective-permute-start.7 = (f32[16,2,512]{2,1,0:T(2,128)S(1)}, f32[16,2,512]{2,1,0:T(2,128)S(1)}, u32[]{:S(2)}, u32[]{:S(2)}) collective-permute-start(f32[16,2,512]{2,1,0:T(2,128)S(1)} %get-tuple-element.12), channel_id=1, source_target_pairs={{1,0},{2,1},{3,2},{4,3},{5,4},{6,5},{7,6},{8,7},{9,8},{10,9},{11,1... | collective-permute-start | bytes 196616 | tf_op jit(solution)/shard_map/ppermute | solution.py:21
  110.4 1.3 collective-permute-done.7
  111.7 0.1 pad_maximum_fusion.11
  111.8 0.1 slice_subtract_fusion
  111.9 0.2 minimum_add_fusion
  112.1 0.4 fusion.6
  112.5 0.2 fusion.36
  112.8 0.2 reshape.46
  112.9 0.2 copy.20
  113.1 21.4 %all_to_all.50 = bf16[16,64,128]{2,0,1:T(8,128)(2,1)S(1)} all-to-all(bf16[16,64,128]{2,0,1:T(8,128)(2,1)S(1)} %copy.20), channel_id=1, replica_groups=mesh['vel'=64,'space'=16] {'vel'}, dimensions={1} | all-to-all | bytes 524288 | tf_op jit(solution)/shard_map/all_to_all | solution.py:82
  134.5 0.8 fusion.45
  135.3 0.8 fusion.2
  136.2 0.8 reduce.1
  137.0 0.2 copy.25
  137.2 0.1 reshape.55
  137.3 19.7 %all_to_all.51 = bf16[64,2,1024]{2,1,0:T(2,128)(2,1)} all-to-all(bf16[64,2,1024]{2,1,0:T(2,128)(2,1)S(1)} %reshape.55), channel_id=1, replica_groups=mesh['vel'=64,'space'=16] {'vel'}, dimensions={0} | all-to-all | bytes 524288 | tf_op jit(solution)/shard_map/all_to_all | solution.py:80
  157.0 2.1 %reshape.56 = bf16[1024,1,128]{2,1,0:T(2,128)(2,1)S(1)} reshape(bf16[64,2,1024]{2,1,0:T(2,128)(2,1)} %all_to_all.51) | data formatting | bytes 524288
  159.2 1.0 copy.23
  160.1 1.1 reshape.50
  161.3 0.9 multiply_add_fusion
  (19 shorter events, 0.3 us)
Async XLA Ops:
  0.0 64.2 %copy-start = (bf16[1024,1024]{1,0:T(8,128)(2,1)S(1)}, bf16[1024,1024]{1,0:T(8,128)(2,1)}, u32[]{:S(2)}) copy-start(bf16[1024,1024]{1,0:T(8,128)(2,1)} %param.7) | copy-start | bytes 6291460
  1.2 12.1 %collective-permute-start = (f32[16,2,512]{2,1,0:T(2,128)S(1)}, f32[16,2,512]{2,1,0:T(2,128)S(1)}, u32[]{:S(2)}, u32[]{:S(2)}) collective-permute-start(f32[16,2,512]{2,1,0:T(2,128)S(1)} %get-tuple-element.17), channel_id=1, source_target_pairs={{0,1},{1,2},{2,3},{3,4},{4,5},{5,6},{6,7},{7,8},{8,9},{9,10},{10,1... | collective-permute-start | bytes 196616 | tf_op jit(solution)/shard_map/ppermute | solution.py:18
  7.0 6.9 %collective-permute-start.1 = (f32[16,2,512]{2,1,0:T(2,128)S(1)}, f32[16,2,512]{2,1,0:T(2,128)S(1)}, u32[]{:S(2)}, u32[]{:S(2)}) collective-permute-start(f32[16,2,512]{2,1,0:T(2,128)S(1)} %get-tuple-element.18), channel_id=1, source_target_pairs={{1,0},{2,1},{3,2},{4,3},{5,4},{6,5},{7,6},{8,7},{9,8},{10,9},{11,1... | collective-permute-start | bytes 196616 | tf_op jit(solution)/shard_map/ppermute | solution.py:21
  15.1 1.0 copy-start.1
  16.8 7.8 %collective-permute-start.2 = (f32[16,2,512]{2,1,0:T(2,128)S(1)}, f32[16,2,512]{2,1,0:T(2,128)S(1)}, u32[]{:S(2)}, u32[]{:S(2)}) collective-permute-start(f32[16,2,512]{2,1,0:T(2,128)S(1)} %get-tuple-element.15), channel_id=1, source_target_pairs={{0,1},{1,2},{2,3},{3,4},{4,5},{5,6},{6,7},{7,8},{8,9},{9,10},{10,1... | collective-permute-start | bytes 196616 | tf_op jit(solution)/shard_map/ppermute | solution.py:18
  18.7 7.1 %collective-permute-start.3 = (f32[16,2,512]{2,1,0:T(2,128)S(1)}, f32[16,2,512]{2,1,0:T(2,128)S(1)}, u32[]{:S(2)}, u32[]{:S(2)}) collective-permute-start(f32[16,2,512]{2,1,0:T(2,128)S(1)} %get-tuple-element.16), channel_id=1, source_target_pairs={{1,0},{2,1},{3,2},{4,3},{5,4},{6,5},{7,6},{8,7},{9,8},{10,9},{11,1... | collective-permute-start | bytes 196616 | tf_op jit(solution)/shard_map/ppermute | solution.py:21
  27.1 38.0 %copy-start.2 = (bf16[1024,1024]{1,0:T(8,128)(2,1)S(1)}, bf16[1024,1024]{1,0:T(8,128)(2,1)}, u32[]{:S(2)}) copy-start(bf16[1024,1024]{1,0:T(8,128)(2,1)} %param.8) | copy-start | bytes 6291460
  87.4 4.3 %copy-start.4 = (f32[16,512]{1,0:T(8,128)S(1)}, f32[16,512]{1,0:T(8,128)}, u32[]{:S(2)}) copy-start(f32[16,512]{1,0:T(8,128)} %param.9) | copy-start | bytes 98308
  91.9 8.3 %collective-permute-start.4 = (f32[16,2,512]{2,1,0:T(2,128)S(1)}, f32[16,2,512]{2,1,0:T(2,128)S(1)}, u32[]{:S(2)}, u32[]{:S(2)}) collective-permute-start(f32[16,2,512]{2,1,0:T(2,128)S(1)} %get-tuple-element.13), channel_id=1, source_target_pairs={{0,1},{1,2},{2,3},{3,4},{4,5},{5,6},{6,7},{7,8},{8,9},{9,10},{10,1... | collective-permute-start | bytes 196616 | tf_op jit(solution)/shard_map/ppermute | solution.py:18
  94.1 7.1 %collective-permute-start.5 = (f32[16,2,512]{2,1,0:T(2,128)S(1)}, f32[16,2,512]{2,1,0:T(2,128)S(1)}, u32[]{:S(2)}, u32[]{:S(2)}) collective-permute-start(f32[16,2,512]{2,1,0:T(2,128)S(1)} %get-tuple-element.14), channel_id=1, source_target_pairs={{1,0},{2,1},{3,2},{4,3},{5,4},{6,5},{7,6},{8,7},{9,8},{10,9},{11,1... | collective-permute-start | bytes 196616 | tf_op jit(solution)/shard_map/ppermute | solution.py:21
  102.2 8.1 %collective-permute-start.6 = (f32[16,2,512]{2,1,0:T(2,128)S(1)}, f32[16,2,512]{2,1,0:T(2,128)S(1)}, u32[]{:S(2)}, u32[]{:S(2)}) collective-permute-start(f32[16,2,512]{2,1,0:T(2,128)S(1)} %get-tuple-element.11), channel_id=1, source_target_pairs={{0,1},{1,2},{2,3},{3,4},{4,5},{5,6},{6,7},{7,8},{8,9},{9,10},{10,1... | collective-permute-start | bytes 196616 | tf_op jit(solution)/shard_map/ppermute | solution.py:18
  104.2 7.5 %collective-permute-start.7 = (f32[16,2,512]{2,1,0:T(2,128)S(1)}, f32[16,2,512]{2,1,0:T(2,128)S(1)}, u32[]{:S(2)}, u32[]{:S(2)}) collective-permute-start(f32[16,2,512]{2,1,0:T(2,128)S(1)} %get-tuple-element.12), channel_id=1, source_target_pairs={{1,0},{2,1},{3,2},{4,3},{5,4},{6,5},{7,6},{8,7},{9,8},{10,9},{11,1... | collective-permute-start | bytes 196616 | tf_op jit(solution)/shard_map/ppermute | solution.py:21
  112.9 22.4 %copy-start.3 = (bf16[1024,1024]{1,0:T(8,128)(2,1)S(1)}, bf16[1024,1024]{1,0:T(8,128)(2,1)}, u32[]{:S(2)}) copy-start(bf16[1024,1024]{1,0:T(8,128)(2,1)} %param.8) | copy-start | bytes 6291460
where the time goes:
time: 164 us; the launch traced here: 162 us
  blocking collectives  97.8 us (60%)
  starting transfers between devices  35.1 us (21%)
  local copies, waits for them, and re-layouts  12.4 us (8%)
  other arithmetic  8.7 us (5%)
  waiting for transfers between devices  4.45 us (3%)
  matrix products  3.33 us (2%)
    all_to_all x2, blocking collectives, body(): lax.all_to_all(grouped, 'vel', split_axis=1, concat_axis=0, tiled=True)  58.3 us
    all_to_all x2, blocking collectives, body(): lax.all_to_all(collide(lax.all_to_all(grouped, 'vel', split_axis=1, conca...  39.5 us
    ppermute x4, starting transfers between devices, with_halo(): lax.ppermute(lax.slice_in_dim(block, 0, width, axis=dim), axis, backward)  23.4 us
    ppermute x4, starting transfers between devices, with_halo(): lax.ppermute(lax.slice_in_dim(block, block.shape[dim] - width, None, axis...  11.7 us
    unnamed x16, local copies, waits for them, and re-layouts  5.48 us
    convert_element_type x4, local copies, waits for them, and re-layouts, update(): gained.astype(jnp.float32) - rate * rounded.astype(jnp.float32)  4.17 us
    ppermute x4, waiting for transfers between devices, with_halo(): lax.ppermute(lax.slice_in_dim(block, 0, width, axis=dim), axis, backward)  4.06 us
  transfers between devices with their start and end apart: 8, of which 5 were waited for; matrix products, arithmetic and copies ran while one was open for 0% of the time, Pallas kernels for 0%

commit v1 on v0

v1 whole, which is shorter than its diff:
```python
import functools

import jax
import jax.numpy as jnp
from jax import lax
from jax.experimental import pallas as pl
from jax.experimental.pallas import tpu as pltpu
from jax.sharding import PartitionSpec as P

STEPS = 2
TIME_STEP = 0.2
MESH = pl.DeviceIdType.MESH
F32 = jnp.float32
BF16 = jnp.bfloat16
RING = 8
LANES = 128
GROUP = 16
PB = 8
SLAB = 32
HALO = 4
HALF = 512

OFFSETS = sorted(
    [(dx, dz) for dx in range(RING) for dz in range(RING) if (dx, dz) != (0, 0)],
    key=lambda o: -(min(o[0], RING - o[0]) + min(o[1], RING - o[1])),
)


def coords():
    vel, space = lax.axis_index("vel"), lax.axis_index("space")
    z_hi, x, core = vel // 16, (vel // 2) % 8, vel % 2
    y, z_lo = space // 2, space % 2
    return x, y, z_hi, z_lo, core


def device(x, y, z, core):
    return {"vel": (z // 2) * 16 + x * 2 + core, "space": y * 2 + z % 2}


def swap_groups(tiles):
    lane = lax.broadcasted_iota(jnp.int32, (8, LANES), 1) // GROUP
    tiles = list(tiles)
    for bit in (4, 2, 1):
        low = (lane & bit) == 0
        for i in range(8):
            if i & bit:
                continue
            j = i | bit
            a, b = tiles[i], tiles[j]
            tiles[i] = jnp.where(low, a, pltpu.roll(b, bit * GROUP, 1))
            tiles[j] = jnp.where(low, pltpu.roll(a, LANES - bit * GROUP, 1), b)
    return tiles


def minmod(a, b):
    return jnp.maximum(jnp.minimum(a, b), 0.0) + jnp.minimum(jnp.maximum(a, b), 0.0)


def sweep(values, up, down, ahead, behind):
    n = len(values)
    differ = [values[i + 1] - values[i] for i in range(n - 1)]
    slopes = [None] + [minmod(differ[i], differ[i - 1]) for i in range(1, n - 1)]
    fluxes = {}
    for i in range(1, n - 2):
        fluxes[i] = up * (values[i] + ahead * slopes[i]) + down * (
            values[i + 1] - behind * slopes[i + 1]
        )
    return {i: fluxes[i] - fluxes[i - 1] for i in range(2, n - 2)}


def kernel(
    dist_ref, cour_ref, gain_ref, prod_ref, rate_ref, out_ref,
    sin, send, recv, state, smooth, ownr, parr, halo, raw, turned, first, second,
    cour, rates, rate_cols, rate_b, sout, outr,
    in_sem, mat_sem, a2a_ss, a2a_rs, halo_ss, halo_rs, core_ss, core_rs,
    rate_sem, out_ss, out_rs,
):
    x, y, z_hi, z_lo, core = coords()
    z = z_hi * 2 + z_lo
    block = x * RING + z
    up_dev = device(x, lax.rem(y + 1, RING), z, core)
    down_dev = device(x, lax.rem(y + RING - 1, RING), z, core)
    twin = device(x, y, z, 1 - core)
    level = device(x, y, z_hi * 2 + 1 - z_lo, core)

    def far(o):
        return lax.rem(x + o[0], RING), lax.rem(z + o[1], RING)

    barrier = pltpu.get_barrier_semaphore()
    for o in OFFSETS:
        xx, zz = far(o)
        pl.semaphore_signal(barrier, 1, device_id=device(xx, y, zz, core), device_id_type=MESH)
    for peer in (up_dev, down_dev, twin):
        pl.semaphore_signal(barrier, 1, device_id=peer, device_id_type=MESH)

    load = pltpu.make_async_copy(dist_ref, sin, in_sem)
    load.start()
    mats = [
        pltpu.make_async_copy(gain_ref.at[:, core], raw.at[0], mat_sem.at[0]),
        pltpu.make_async_copy(prod_ref.at[:, core], raw.at[1], mat_sem.at[1]),
    ]
    for m in mats:
        m.start()
    load.wait()

    for h in range(2):
        for q in range(4):
            rows = jnp.concatenate(
                [sin[:, h * 8 + i, q * LANES:(q + 1) * LANES] for i in range(8)], axis=0
            )
            send[h, q * 16:(q + 1) * 16] = rows.T.reshape(16, PB, LANES)

    speeds = cour_ref[...]
    lane = lax.broadcasted_iota(jnp.int32, (8, LANES), 1)
    even = jnp.zeros((8, LANES), F32)
    odd = jnp.zeros((8, LANES), F32)
    for i in range(4):
        for is_odd in range(2):
            target = (is_odd * 4 + i) * GROUP
            shifts = [(target - i * 32 - cc * GROUP) % LANES for cc in range(2)]
            rolled = [pltpu.roll(speeds, s, 1) if s else speeds for s in shifts]
            here = (lane // GROUP) == (is_odd * 4 + i)
            piece = jnp.where(core == 0, rolled[0], rolled[1])
            if is_odd:
                odd = jnp.where(here, piece, odd)
            else:
                even = jnp.where(here, piece, even)
    for t in range(4):
        row = jnp.where(lane < 64, even[2 * t:2 * t + 1], odd[2 * t + 1:2 * t + 2])
        cour[t] = row

    pl.semaphore_wait(barrier, len(OFFSETS) + 3)

    rate_copy = pltpu.make_async_remote_copy(
        rate_ref, rates.at[z_lo], rate_sem.at[0], rate_sem.at[1], device_id=level, device_id_type=MESH
    )
    for phase in range(2):
        h = z_lo if phase == 0 else 1 - z_lo
        for o in OFFSETS:
            xx, zz = far(o)
            pltpu.make_async_remote_copy(
                send.at[h, xx * RING + zz], recv.at[phase, z_lo, z_hi, x],
                a2a_ss.at[phase], a2a_rs.at[phase],
                device_id=device(xx, y, zz, core), device_id_type=MESH,
            ).start()
        pltpu.make_async_copy(
            send.at[h, block], recv.at[phase, z_lo, z_hi, x], a2a_rs.at[phase]
        ).start()
        if phase == 0:
            rate_copy.start()

    m_at = lax.broadcasted_iota(jnp.int32, (256, 256), 0)
    n_at = lax.broadcasted_iota(jnp.int32, (256, 256), 1)
    whose = jnp.where(m_at < LANES, core, 1 - core)
    inner = m_at % LANES
    pick = (n_at == (inner // GROUP) * 32 + whose * GROUP + inner % GROUP).astype(F32).astype(BF16)
    for k in range(2):
        mats[k].wait()
        for b in range(4):
            block_cols = raw[k, :, :, b * 256:(b + 1) * 256].reshape(HALF, 256)
            res = lax.dot_general(
                pick, block_cols, (((1,), (1,)), ((), ())), preferred_element_type=F32
            ).astype(BF16)
            turned[k, b * LANES:(b + 1) * LANES] = res[:LANES]
            turned[k, HALF + b * LANES:HALF + (b + 1) * LANES] = res[LANES:]

    rates[z_lo] = rate_ref[...]
    rate_copy.wait()
    rate_cols[...] = jnp.zeros_like(rate_cols)
    cell_tile = pl.multiple_of((block // 16) * LANES, LANES)
    rate_cols[0:16] = rates[0, :, pl.ds(cell_tile, LANES)]
    rate_cols[16:32] = rates[1, :, pl.ds(cell_tile, LANES)]
    rate_cols[...] = rate_cols[...].T
    column = rate_cols[pl.ds(pl.multiple_of((block % 16) * PB, PB), PB), :]
    for i in range(SLAB):
        rate_b[i] = jnp.broadcast_to(column[:, i:i + 1], (PB, LANES))

    def arrived(phase):
        pltpu.make_async_copy(recv.at[phase], recv.at[phase], a2a_rs.at[phase]).wait()

    def unpack(phase):
        for zl in range(2):
            h = zl if phase == 0 else 1 - zl
            for t in range(4):
                tiles = swap_groups([recv[phase, zl, t, g] for g in range(8)])
                for i in range(8):
                    state[zl * 16 + h * 8 + i, :, t * LANES:(t + 1) * LANES] = tiles[i]

    def halo_copies(step):
        return [
            pltpu.make_async_remote_copy(
                state.at[pl.ds(SLAB - HALO, HALO)], halo.at[step, 0], halo_ss.at[step, 0],
                halo_rs.at[step, 0], device_id=up_dev, device_id_type=MESH,
            ),
            pltpu.make_async_remote_copy(
                state.at[pl.ds(0, HALO)], halo.at[step, 1], halo_ss.at[step, 1],
                halo_rs.at[step, 1], device_id=down_dev, device_id_type=MESH,
            ),
        ]

    arrived(0)
    unpack(0)
    halos = halo_copies(0)
    for c in halos:
        c.start()
    arrived(1)
    unpack(1)

    for step in range(STEPS):
        for c in halos:
            c.wait()
        for t in range(4):
            cols = slice(t * LANES, (t + 1) * LANES)
            c = cour[t]
            up, down = jnp.maximum(c, 0.0), jnp.minimum(c, 0.0)
            ahead, behind = 0.5 * (1.0 - c), 0.5 * (1.0 + c)
            for lo in range(0, SLAB, 16):
                planes = []
                for i in range(lo - HALO, lo + 16 + HALO):
                    if i < 0:
                        planes.append(halo[step, 0, i + HALO, :, cols])
                    elif i >= SLAB:
                        planes.append(halo[step, 1, i - SLAB, :, cols])
                    else:
                        planes.append(state[i, :, cols])
                less = sweep(planes, up, down, ahead, behind)
                section = [planes[i] - less[i] for i in range(2, len(planes) - 2)]
                less2 = sweep(section, up, down, ahead, behind)
                result = [
                    0.5 * planes[i + 2] + 0.5 * (section[i] - less2[i])
                    for i in range(2, len(section) - 2)
                ]
                for i in range(0, 16, 2):
                    smooth[lo + i, :, cols] = result[i]
                    smooth[lo + i + 1, :, cols] = result[i + 1]
                    pair = jnp.concatenate([result[i], result[i + 1]], axis=0)
                    ownr[step, (lo + i) * PB:(lo + i + 2) * PB, cols] = pair.astype(BF16)
        share = pltpu.make_async_remote_copy(
            ownr.at[step], parr.at[step], core_ss.at[step], core_rs.at[step],
            device_id=twin, device_id_type=MESH,
        )
        share.start()
        first[...] = jnp.dot(ownr[step], turned[0, :HALF], preferred_element_type=F32)
        second[...] = jnp.dot(ownr[step], turned[1, :HALF], preferred_element_type=F32)
        share.wait()
        first[...] += jnp.dot(parr[step], turned[0, HALF:], preferred_element_type=F32)
        second[...] += jnp.dot(parr[step], turned[1, HALF:], preferred_element_type=F32)
        for i in range(0, SLAB, 2):
            rows = slice(i * PB, (i + 2) * PB)
            gained = (first[rows] * second[rows]).astype(BF16).astype(F32)
            rounded = ownr[step, rows].astype(F32)
            for j in range(2):
                part = slice(j * PB, (j + 1) * PB)
                rate = jnp.concatenate([rate_b[i + j]] * 4, axis=1)
                state[i + j] = smooth[i + j] + TIME_STEP * (gained[part] - rate * rounded[part])
        if step + 1 < STEPS:
            halos = halo_copies(step + 1)
            for c in halos:
                c.start()

    for zl in range(2):
        for h in range(2):
            for t in range(4):
                tiles = swap_groups(
                    [state[zl * 16 + h * 8 + i, :, t * LANES:(t + 1) * LANES] for i in range(8)]
                )
                for g in range(8):
                    sout[h, g, t * 2 + zl] = tiles[g]
    for h in range(2):
        for o in OFFSETS:
            xx, zz = far(o)
            pltpu.make_async_remote_copy(
                sout.at[h, xx, zz], outr.at[h, block], out_ss.at[h], out_rs.at[h],
                device_id=device(xx, y, zz, core), device_id_type=MESH,
            ).start()
        pltpu.make_async_copy(sout.at[h, x, z], outr.at[h, block], out_rs.at[h]).start()
    for h in range(2):
        pltpu.make_async_copy(outr.at[h], outr.at[h], out_rs.at[h]).wait()
        for q in range(4):
            rows = outr[h, q * 16:(q + 1) * 16].reshape(LANES, LANES).T
            out_ref[h * 8:(h + 1) * 8, :, q * LANES:(q + 1) * LANES] = rows.reshape(8, 16, LANES)
    for phase in range(2):
        sent = send.at[0, pl.ds(0, len(OFFSETS))]
        pltpu.make_async_copy(sent, sent, a2a_ss.at[phase]).wait()
        pltpu.make_async_copy(sent, sent, out_ss.at[phase]).wait()


def body(distribution, courant, gain_matrix, product_matrix, collision_rate):
    dma = pltpu.SemaphoreType.DMA
    planes = pl.pallas_call(
        kernel,
        out_shape=jax.ShapeDtypeStruct((16, GROUP, 512), F32),
        in_specs=[
            pl.BlockSpec(memory_space=pl.ANY),
            pl.BlockSpec(memory_space=pltpu.VMEM),
            pl.BlockSpec(memory_space=pl.ANY),
            pl.BlockSpec(memory_space=pl.ANY),
            pl.BlockSpec(memory_space=pltpu.VMEM),
        ],
        out_specs=pl.BlockSpec(memory_space=pltpu.VMEM),
        scratch_shapes=[
            pltpu.VMEM((GROUP, 16, 512), F32),
            pltpu.VMEM((2, 64, PB, LANES), F32),
            pltpu.VMEM((2, 2, 4, 8, PB, LANES), F32),
            pltpu.VMEM((SLAB, PB, HALF), F32),
            pltpu.VMEM((SLAB, PB, HALF), F32),
            pltpu.VMEM((STEPS, SLAB * PB, HALF), BF16),
            pltpu.VMEM((STEPS, SLAB * PB, HALF), BF16),
            pltpu.VMEM((STEPS, 2, HALO, PB, HALF), F32),
            pltpu.VMEM((2, 32, GROUP, 1024), BF16),
            pltpu.VMEM((2, 1024, HALF), BF16),
            pltpu.VMEM((SLAB * PB, HALF), F32),
            pltpu.VMEM((SLAB * PB, HALF), F32),
            pltpu.VMEM((4, 8, LANES), F32),
            pltpu.VMEM((2, 16, 512), F32),
            pltpu.VMEM((LANES, LANES), F32),
            pltpu.VMEM((SLAB, PB, LANES), F32),
            pltpu.VMEM((2, 8, 8, PB, LANES), F32),
            pltpu.VMEM((2, 64, PB, LANES), F32),
            dma, dma((2,)), dma((2,)), dma((2,)), dma((STEPS, 2)), dma((STEPS, 2)),
            dma((STEPS,)), dma((STEPS,)), dma((2,)), dma((2,)), dma((2,)),
        ],
        compiler_params=pltpu.CompilerParams(collective_id=0, has_side_effects=True),
        name="boltzmann",
    )(
        distribution,
        courant.reshape(8, LANES),
        gain_matrix.reshape(32, 2, GROUP, 1024),
        product_matrix.reshape(32, 2, GROUP, 1024),
        collision_rate,
    )
    return jnp.transpose(planes, (1, 0, 2))


def solution(mesh):
    in_specs = (P("vel", "space", None), P(), P(), P(), P("space", None))
    out_specs = P("vel", "space", None)
    return jax.shard_map(body, mesh=mesh, in_specs=in_specs, out_specs=out_specs, check_vma=False)
```

time: 164 us -> 70.6 us (0.43)
  blocking collectives: 97.8 us -> 0 us
  Pallas kernels: 0 us -> 68.1 us
  starting transfers between devices: 35.1 us -> 0 us
  local copies, waits for them, and re-layouts: 12.4 us -> 2.14 us
  other arithmetic: 8.7 us -> 0 us
  waiting for transfers between devices: 4.45 us -> 0 us
  matrix products: 3.33 us -> 0 us
    all_to_all x4 -> x0, blocking collectives: 97.8 us -> none  [the longest x2 58.3 us: body(): lax.all_to_all(grouped, 'vel', split_axis=1, concat_axis=0, tiled=True)]
    pallas_call x0 -> x1, Pallas kernels: none -> 68.1 us  [body(): pl.pallas_call(kernel, out_shape=jax.ShapeDtypeStruct((16, GROUP, 512), F...]
    ppermute x8 -> x0, starting transfers between devices: 35.1 us -> none  [the longest x4 23.4 us: with_halo(): lax.ppermute(lax.slice_in_dim(block, 0, width, axis=dim), axis, backward)]
    unnamed x16 -> x0, local copies, waits for them, and re-layouts: 5.48 us -> none
    ppermute x8 -> x0, waiting for transfers between devices: 4.45 us -> none  [the longest x4 4.06 us: with_halo(): lax.ppermute(lax.slice_in_dim(block, 0, width, axis=dim), axis, backward)]
    convert_element_type x4 -> x0, local copies, waits for them, and re-layouts: 4.17 us -> none  [update(): gained.astype(jnp.float32) - rate * rounded.astype(jnp.float32)]
    add x12 -> x0, other arithmetic: 3.77 us -> none  [the longest x4 1.67 us: change(): upward * (left_value + 0.5 * (1.0 - speeds) * left_slope)]
    dot_general x4 -> x0, matrix products: 3.33 us -> none  [the longest x2 1.67 us: collide(): jnp.dot(gain_matrix, columns, preferred_element_type=jnp.float32)]
  transfers between devices with their start and end apart: 8 -> 0, of which waited for: 5 -> 0; matrix products, arithmetic and copies ran while one was open for 0% -> 0% of each run, Pallas kernels for 0% -> 0%
where the time goes in v1:
time: 70.6 us; the launch traced here: 70.3 us
  Pallas kernels  68.1 us (96%)
  local copies, waits for them, and re-layouts  2.14 us (3%)
    pallas_call x1, Pallas kernels, body(): pl.pallas_call(kernel, out_shape=jax.ShapeDtypeStruct((16, GROUP, 512), F...  68.1 us
    transpose x1, local copies, waits for them, and re-layouts, body(): return jnp.transpose(planes, (1, 0, 2))  2.14 us

profile of v1, /device:TPU:1, one launch (start us, length us, event | category | flops | bytes accessed | tf_op | source)
XLA Modules:
  0.0 70.3 jit_solution(12538873437071086420)
XLA Ops:
  0.0 68.1 %boltzmann.1 = f32[16,16,512]{2,1,0:T(8,128)} custom-call(f32[16,16,512]{2,1,0:T(8,128)} %dist_ref.1, f32[8,128]{1,0:T(8,128)} %bitcast.7, bf16[32,2,16,1024]{3,2,1,0:T(8,128)(2,1)} %bitcast.5, bf16[32,2,16,1024]{3,2,1,0:T(8,128)(2,1)} %bitcast.6, f32[16,512]{1,0:T(8,128)} %rate_ref.1), custom_call_target="tpu_custom_call" | custom-call | tf_op jit(solution)/shard_map/boltzmann/pallas_call | solution.py:290
  68.1 2.1 %copy.6 = f32[16,16,512]{2,1,0:T(8,128)} copy(f32[16,16,512]{2,0,1:T(8,128)} %bitcast.4) | data formatting | bytes 1048576 | tf_op jit(solution)/shard_map/transpose | solution.py:332

commit v2 on v1

v2 whole, which is shorter than its diff:
```python
import functools

import jax
import jax.numpy as jnp
from jax import lax
from jax.experimental import pallas as pl
from jax.experimental.pallas import tpu as pltpu
from jax.sharding import PartitionSpec as P

STEPS = 2
TIME_STEP = 0.2
MESH = pl.DeviceIdType.MESH
F32 = jnp.float32
BF16 = jnp.bfloat16
RING = 8
LANES = 128
GROUP = 16
PB = 8
SLAB = 32
HALO = 4
SPAN = 2.0 ** 30
HALF = 512

OFFSETS = sorted(
    [(dx, dz) for dx in range(RING) for dz in range(RING) if (dx, dz) != (0, 0)],
    key=lambda o: -(min(o[0], RING - o[0]) + min(o[1], RING - o[1])),
)
BACK = sorted(
    [(j, dx) for j in range(4) for dx in range(RING)],
    key=lambda o: -(min(2 * o[0], RING - 2 * o[0]) + min(o[1], RING - o[1])),
)


def coords():
    vel, space = lax.axis_index("vel"), lax.axis_index("space")
    z_hi, x, core = vel // 16, (vel // 2) % 8, vel % 2
    y, z_lo = space // 2, space % 2
    return x, y, z_hi, z_lo, core


def device(x, y, z, core):
    return {"vel": (z // 2) * 16 + x * 2 + core, "space": y * 2 + z % 2}


def swap_groups(tiles):
    lane = lax.broadcasted_iota(jnp.int32, (8, LANES), 1) // GROUP
    tiles = list(tiles)
    for bit in (4, 2, 1):
        low = (lane & bit) == 0
        for i in range(8):
            if i & bit:
                continue
            j = i | bit
            a, b = tiles[i], tiles[j]
            tiles[i] = jnp.where(low, a, pltpu.roll(b, bit * GROUP, 1))
            tiles[j] = jnp.where(low, pltpu.roll(a, LANES - bit * GROUP, 1), b)
    return tiles


def encode(values):
    square = values * values
    power = square * square
    return jnp.where(values < 0.0, -power, power)


def decode(powers):
    root = jnp.sqrt(jnp.sqrt(jnp.abs(powers)))
    return jnp.where(powers < 0.0, -root, root)


def minmod(a, b):
    return jnp.maximum(jnp.minimum(a, b), 0.0) + jnp.minimum(jnp.maximum(a, b), 0.0)


def sweep(values, up, down, ahead, behind):
    n = len(values)
    differ = [values[i + 1] - values[i] for i in range(n - 1)]
    slopes = [None] + [minmod(differ[i], differ[i - 1]) for i in range(1, n - 1)]
    fluxes = {}
    for i in range(1, n - 2):
        fluxes[i] = up * (values[i] + ahead * slopes[i]) + down * (
            values[i + 1] - behind * slopes[i + 1]
        )
    return {i: fluxes[i] - fluxes[i - 1] for i in range(2, n - 2)}


def kernel(
    dist_ref, cour_ref, gain_ref, prod_ref, rate_ref, out_ref, unit_ref,
    sin, send, recv, state, later, smooth, ownr, parr, halo, raw, turned, first, second,
    cour, rates, rate_cols, rate_b, sout, sunit,
    in_sem, mat_sem, a2a_ss, a2a_rs, halo_ss, halo_rs, core_ss, core_rs,
    rate_sem, out_ss, out_rs, unit_ss, unit_rs,
):
    x, y, z_hi, z_lo, core = coords()
    z = z_hi * 2 + z_lo
    block = x * RING + z
    up_dev = device(x, lax.rem(y + 1, RING), z, core)
    down_dev = device(x, lax.rem(y + RING - 1, RING), z, core)
    twin = device(x, y, z, 1 - core)
    level = device(x, y, z_hi * 2 + 1 - z_lo, core)

    turn = 1 - 2 * core

    def far(o):
        return lax.rem(x + RING + turn * o[0], RING), lax.rem(z + RING + turn * o[1], RING)

    barrier = pltpu.get_barrier_semaphore()
    for o in OFFSETS:
        xx, zz = far(o)
        pl.semaphore_signal(barrier, 1, device_id=device(xx, y, zz, core), device_id_type=MESH)
    for peer in (up_dev, down_dev, twin):
        pl.semaphore_signal(barrier, 1, device_id=peer, device_id_type=MESH)

    load = pltpu.make_async_copy(dist_ref, sin, in_sem)
    load.start()
    mats = [
        pltpu.make_async_copy(gain_ref.at[:, core], raw.at[0], mat_sem.at[0]),
        pltpu.make_async_copy(prod_ref.at[:, core], raw.at[1], mat_sem.at[1]),
    ]
    for m in mats:
        m.start()
    load.wait()

    for h in range(2):
        for q in range(4):
            rows = jnp.concatenate(
                [sin[:, h * 8 + i, q * LANES:(q + 1) * LANES] for i in range(8)], axis=0
            )
            send[h, q * 16:(q + 1) * 16] = rows.T.reshape(16, PB, LANES)

    pl.semaphore_wait(barrier, len(OFFSETS) + 3)

    rate_copy = pltpu.make_async_remote_copy(
        rate_ref, rates.at[z_lo], rate_sem.at[0], rate_sem.at[1], device_id=level, device_id_type=MESH
    )
    def send_phase(phase):
        h = z_lo if phase == 0 else 1 - z_lo
        for o in OFFSETS:
            xx, zz = far(o)
            pltpu.make_async_remote_copy(
                send.at[h, xx * RING + zz], recv.at[phase, z_lo, z_hi, x],
                a2a_ss.at[phase], a2a_rs.at[phase],
                device_id=device(xx, y, zz, core), device_id_type=MESH,
            ).start()
        pltpu.make_async_copy(
            send.at[h, block], recv.at[phase, z_lo, z_hi, x], a2a_rs.at[phase]
        ).start()

    rate_copy.start()
    send_phase(0)

    speeds = cour_ref[...]
    lane = lax.broadcasted_iota(jnp.int32, (8, LANES), 1)
    even = jnp.zeros((8, LANES), F32)
    odd = jnp.zeros((8, LANES), F32)
    for i in range(4):
        for is_odd in range(2):
            target = (is_odd * 4 + i) * GROUP
            shifts = [(target - i * 32 - cc * GROUP) % LANES for cc in range(2)]
            rolled = [pltpu.roll(speeds, s, 1) if s else speeds for s in shifts]
            here = (lane // GROUP) == (is_odd * 4 + i)
            piece = jnp.where(core == 0, rolled[0], rolled[1])
            if is_odd:
                odd = jnp.where(here, piece, odd)
            else:
                even = jnp.where(here, piece, even)
    for t in range(4):
        cour[t] = jnp.where(lane < 64, even[2 * t:2 * t + 1], odd[2 * t + 1:2 * t + 2])

    m_at = lax.broadcasted_iota(jnp.int32, (256, 256), 0)
    n_at = lax.broadcasted_iota(jnp.int32, (256, 256), 1)
    whose = jnp.where(m_at < LANES, core, 1 - core)
    inner = m_at % LANES
    pick = (n_at == (inner // GROUP) * 32 + whose * GROUP + inner % GROUP).astype(F32).astype(BF16)
    for k in range(2):
        mats[k].wait()
        for b in range(4):
            block_cols = raw[k, :, :, b * 256:(b + 1) * 256].reshape(HALF, 256)
            res = lax.dot_general(
                pick, block_cols, (((1,), (1,)), ((), ())), preferred_element_type=F32
            ).astype(BF16)
            turned[k, b * LANES:(b + 1) * LANES] = res[:LANES]
            turned[k, HALF + b * LANES:HALF + (b + 1) * LANES] = res[LANES:]

    def spread_rates():
        rates[z_lo] = rate_ref[...]
        rate_copy.wait()
        rate_cols[...] = jnp.zeros_like(rate_cols)
        cell_tile = pl.multiple_of((block // 16) * LANES, LANES)
        rate_cols[0:16] = rates[0, :, pl.ds(cell_tile, LANES)]
        rate_cols[16:32] = rates[1, :, pl.ds(cell_tile, LANES)]
        rate_cols[...] = rate_cols[...].T
        column = rate_cols[pl.ds(pl.multiple_of((block % 16) * PB, PB), PB), :]
        for i in range(SLAB):
            rate_b[i] = jnp.broadcast_to(column[:, i:i + 1], (PB, LANES))

    def arrived(phase):
        pltpu.make_async_copy(recv.at[phase], recv.at[phase], a2a_rs.at[phase]).wait()

    def unpack(phase):
        for zl in range(2):
            h = zl if phase == 0 else 1 - zl
            for t in range(4):
                tiles = swap_groups([recv[phase, zl, t, g] for g in range(8)])
                for i in range(8):
                    state[zl * 16 + h * 8 + i, :, t * LANES:(t + 1) * LANES] = tiles[i]

    def send_faces(source, step):
        copies = [
            pltpu.make_async_remote_copy(
                source.at[pl.ds(SLAB - HALO, HALO)], halo.at[step, 0], halo_ss.at[step, 0],
                halo_rs.at[step, 0], device_id=up_dev, device_id_type=MESH,
            ),
            pltpu.make_async_remote_copy(
                source.at[pl.ds(0, HALO)], halo.at[step, 1], halo_ss.at[step, 1],
                halo_rs.at[step, 1], device_id=down_dev, device_id_type=MESH,
            ),
        ]
        for c in copies:
            c.start()
        return copies

    def advect(source, step, lo, count):
        for t in range(4):
            cols = slice(t * LANES, (t + 1) * LANES)
            c = cour[t]
            up, down = jnp.maximum(c, 0.0), jnp.minimum(c, 0.0)
            ahead, behind = 0.5 * (1.0 - c), 0.5 * (1.0 + c)
            planes = []
            for i in range(lo - HALO, lo + count + HALO):
                if i < 0:
                    planes.append(halo[step, 0, i + HALO, :, cols])
                elif i >= SLAB:
                    planes.append(halo[step, 1, i - SLAB, :, cols])
                else:
                    planes.append(source[i, :, cols])
            less = sweep(planes, up, down, ahead, behind)
            section = [planes[i] - less[i] for i in range(2, len(planes) - 2)]
            less2 = sweep(section, up, down, ahead, behind)
            result = [
                0.5 * planes[i + 2] + 0.5 * (section[i] - less2[i])
                for i in range(2, len(section) - 2)
            ]
            for i in range(0, count, 2):
                smooth[lo + i, :, cols] = result[i]
                smooth[lo + i + 1, :, cols] = result[i + 1]
                pair = jnp.concatenate([result[i], result[i + 1]], axis=0)
                ownr[step, (lo + i) * PB:(lo + i + 2) * PB, cols] = pair.astype(BF16)

    def share(step, number, lo, count):
        rows = pl.ds(lo * PB, count * PB)
        copy = pltpu.make_async_remote_copy(
            ownr.at[step, rows], parr.at[step, rows], core_ss.at[number], core_rs.at[number],
            device_id=twin, device_id_type=MESH,
        )
        copy.start()
        return copy

    def rows_of(ref, step, ranges):
        parts = [ref[step, lo * PB:(lo + count) * PB] for lo, count in ranges]
        return parts[0] if len(parts) == 1 else jnp.concatenate(parts, axis=0)

    def products(source, step, ranges, half, add):
        block_rows = rows_of(source, step, ranges)
        for k, total in ((0, first), (1, second)):
            value = jnp.dot(
                block_rows, turned[k, half * HALF:(half + 1) * HALF], preferred_element_type=F32
            )
            at = 0
            for lo, count in ranges:
                rows = slice(lo * PB, (lo + count) * PB)
                part = value[at:at + count * PB]
                total[rows] = total[rows] + part if add else part
                at += count * PB

    def update(target, step, ranges):
        for lo, count in ranges:
            for i in range(lo, lo + count, 2):
                rows = slice(i * PB, (i + 2) * PB)
                gained = (first[rows] * second[rows]).astype(BF16).astype(F32)
                rounded = ownr[step, rows].astype(F32)
                for j in range(2):
                    part = slice(j * PB, (j + 1) * PB)
                    rate = jnp.concatenate([rate_b[i + j]] * 4, axis=1)
                    target[i + j] = smooth[i + j] + TIME_STEP * (
                        gained[part] - rate * rounded[part]
                    )

    arrived(0)
    send_phase(1)
    unpack(0)
    faces = send_faces(state, 0)
    spread_rates()
    for c in faces:
        c.wait()
    edges = ((0, HALO), (SLAB - HALO, HALO))
    shares = []
    for n, (lo, count) in enumerate(edges):
        advect(state, 0, lo, count)
        shares.append(share(0, n, lo, count))
    products(ownr, 0, edges, 0, False)
    for c in shares:
        c.wait()
    products(parr, 0, edges, 1, True)
    update(later, 0, edges)
    faces = send_faces(later, 1)
    arrived(1)
    unpack(1)
    inside = ((HALO, 12), (HALO + 12, 12))
    shares = []
    for n, (lo, count) in enumerate(inside):
        advect(state, 0, lo, count)
        shares.append(share(0, 2 + n, lo, count))
    inside = ((HALO, 24),)
    products(ownr, 0, inside, 0, False)
    for c in shares:
        c.wait()
    products(parr, 0, inside, 1, True)
    update(later, 0, inside)
    for c in faces:
        c.wait()

    def dispatch(zl):
        odd = lax.rem(z_lo + zl, 2)
        for j, dx in BACK:
            xx, zz = far((dx, 2 * j + odd))
            t = zz // 2

            def remote():
                to = device(xx, y, zz, core)
                pltpu.make_async_remote_copy(
                    sunit.at[zl], unit_ref.at[block], unit_ss, unit_rs,
                    device_id=to, device_id_type=MESH,
                ).start()
                pltpu.make_async_remote_copy(
                    sout.at[zl, xx, t], out_ref.at[block], out_ss, out_rs,
                    device_id=to, device_id_type=MESH,
                ).start()

            if j or dx:
                remote()
            else:
                pl.when(odd == 1)(remote)

                @pl.when(odd == 0)
                def _():
                    pltpu.make_async_copy(sunit.at[zl], unit_ref.at[block], unit_rs).start()
                    pltpu.make_async_copy(sout.at[zl, x, t], out_ref.at[block], out_rs).start()

    shares = []
    for zl in range(2):
        advect(later, 1, zl * 16, 16)
        shares.append(share(1, 4 + zl, zl * 16, 16))
    for zl in range(2):
        part = ((zl * 16, 16),)
        products(ownr, 1, part, 0, False)
        shares[zl].wait()
        products(parr, 1, part, 1, True)
        update(state, 1, part)
        top = jnp.abs(state[zl * 16])
        for i in range(1, 16):
            top = jnp.maximum(top, jnp.abs(state[zl * 16 + i]))
        top = jnp.maximum(jnp.max(top, axis=(0, 1), keepdims=True), 1e-20)
        unit = jnp.broadcast_to(top * (1.0 / SPAN), (PB, LANES)).astype(BF16).astype(F32)
        sunit[zl] = unit[:1]
        scale = 1.0 / unit
        for t in range(4):
            pair = [
                swap_groups(
                    [
                        encode(state[zl * 16 + h * 8 + i, :, t * LANES:(t + 1) * LANES] * scale)
                        for i in range(8)
                    ]
                )
                for h in range(2)
            ]
            for g in range(8):
                sout[zl, g, t] = jnp.concatenate([pair[0][g], pair[1][g]], axis=0).astype(BF16)
        dispatch(zl)

    pltpu.make_async_copy(out_ref, out_ref, out_rs).wait()
    pltpu.make_async_copy(unit_ref, unit_ref, unit_rs).wait()
    sent = out_ref.at[pl.ds(0, len(OFFSETS))]
    pltpu.make_async_copy(sent, sent, out_ss).wait()
    sent = unit_ref.at[pl.ds(0, len(OFFSETS))]
    pltpu.make_async_copy(sent, sent, unit_ss).wait()
    for phase in range(2):
        sent = send.at[0, pl.ds(0, len(OFFSETS))]
        pltpu.make_async_copy(sent, sent, a2a_ss.at[phase]).wait()


def place(tiles_ref, unit_ref, out_ref):
    m_at = lax.broadcasted_iota(jnp.int32, (LANES, LANES), 0)
    n_at = lax.broadcasted_iota(jnp.int32, (LANES, LANES), 1)
    order = (n_at == (m_at % 8) * GROUP + m_at // 8).astype(F32).astype(BF16)
    last = (((1,), (1,)), ((), ()))
    for q in range(4):
        part = slice(q * 16, (q + 1) * 16)
        cols = slice(q * LANES, (q + 1) * LANES)
        units = jnp.broadcast_to(unit_ref[part], (16, PB, LANES)).reshape(LANES, LANES).astype(BF16)
        unit = lax.dot_general(order[:8], units, last, preferred_element_type=F32)
        tiles = tiles_ref[part].astype(F32)
        for h in range(2):
            block = tiles[:, h * PB:(h + 1) * PB].reshape(LANES, LANES).astype(BF16)
            rows = lax.dot_general(order, block, last, preferred_element_type=F32)
            out_ref[:, h * 8:(h + 1) * 8, cols] = decode(rows).reshape(GROUP, 8, LANES) * unit


def body(distribution, courant, gain_matrix, product_matrix, collision_rate):
    dma = pltpu.SemaphoreType.DMA
    tiles, units = pl.pallas_call(
        kernel,
        out_shape=(
            jax.ShapeDtypeStruct((64, 2 * PB, LANES), BF16),
            jax.ShapeDtypeStruct((64, 1, LANES), F32),
        ),
        in_specs=[
            pl.BlockSpec(memory_space=pl.ANY),
            pl.BlockSpec(memory_space=pltpu.VMEM),
            pl.BlockSpec(memory_space=pl.ANY),
            pl.BlockSpec(memory_space=pl.ANY),
            pl.BlockSpec(memory_space=pltpu.VMEM),
        ],
        out_specs=(pl.BlockSpec(memory_space=pl.ANY), pl.BlockSpec(memory_space=pl.ANY)),
        scratch_shapes=[
            pltpu.VMEM((GROUP, 16, 512), F32),
            pltpu.VMEM((2, 64, PB, LANES), F32),
            pltpu.VMEM((2, 2, 4, 8, PB, LANES), F32),
            pltpu.VMEM((SLAB, PB, HALF), F32),
            pltpu.VMEM((SLAB, PB, HALF), F32),
            pltpu.VMEM((SLAB, PB, HALF), F32),
            pltpu.VMEM((STEPS, SLAB * PB, HALF), BF16),
            pltpu.VMEM((STEPS, SLAB * PB, HALF), BF16),
            pltpu.VMEM((STEPS, 2, HALO, PB, HALF), F32),
            pltpu.VMEM((2, 32, GROUP, 1024), BF16),
            pltpu.VMEM((2, 1024, HALF), BF16),
            pltpu.VMEM((SLAB * PB, HALF), F32),
            pltpu.VMEM((SLAB * PB, HALF), F32),
            pltpu.VMEM((4, 8, LANES), F32),
            pltpu.VMEM((2, 16, 512), F32),
            pltpu.VMEM((LANES, LANES), F32),
            pltpu.VMEM((SLAB, PB, LANES), F32),
            pltpu.VMEM((2, 8, 4, 2 * PB, LANES), BF16),
            pltpu.VMEM((2, 1, LANES), F32),
            dma, dma((2,)), dma((2,)), dma((2,)), dma((STEPS, 2)), dma((STEPS, 2)),
            dma((6,)), dma((6,)), dma((2,)), dma, dma, dma, dma,
        ],
        compiler_params=pltpu.CompilerParams(collective_id=0, has_side_effects=True),
        name="boltzmann",
    )(
        distribution,
        courant.reshape(8, LANES),
        gain_matrix.reshape(32, 2, GROUP, 1024),
        product_matrix.reshape(32, 2, GROUP, 1024),
        collision_rate,
    )
    return pl.pallas_call(
        place,
        out_shape=jax.ShapeDtypeStruct((GROUP, 16, 512), F32),
        in_specs=[pl.BlockSpec(memory_space=pltpu.VMEM)] * 2,
        out_specs=pl.BlockSpec(memory_space=pltpu.VMEM),
        name="place",
    )(tiles, units)


def solution(mesh):
    in_specs = (P("vel", "space", None), P(), P(), P(), P("space", None))
    out_specs = P("vel", "space", None)
    return jax.shard_map(body, mesh=mesh, in_specs=in_specs, out_specs=out_specs, check_vma=False)
```

time: 70.6 us -> 60.1 us (0.85)
  Pallas kernels: 68.1 us -> 59.8 us
  local copies, waits for them, and re-layouts: 2.14 us -> 0 us
    pallas_call x1 -> x2, Pallas kernels: 68.1 us -> 59.8 us  [the longest x1 57.5 us: body(): pl.pallas_call(kernel, out_shape=(jax.ShapeDtypeStruct((64, 2 * PB, LANES...]
    transpose x1 -> x0, local copies, waits for them, and re-layouts: 2.14 us -> none  [body(): return jnp.transpose(planes, (1, 0, 2))]
where the time goes in v2:
time: 60.1 us; the launch traced here: 59.8 us
  Pallas kernels  59.8 us (100%)
    pallas_call x1, Pallas kernels, body(): pl.pallas_call(kernel, out_shape=(jax.ShapeDtypeStruct((64, 2 * PB, LANES...  57.5 us
    pallas_call x1, Pallas kernels, body(): pl.pallas_call(place, out_shape=jax.ShapeDtypeStruct((GROUP, 16, 512), F3...  2.28 us

profile of v2, /device:TPU:1, one launch (start us, length us, event | category | flops | bytes accessed | tf_op | source)
XLA Modules:
  0.0 59.8 jit_solution(6086899050052991820)
XLA Ops:
  0.0 57.5 %boltzmann.1 = (bf16[64,16,128]{2,1,0:T(8,128)(2,1)}, f32[64,1,128]{2,1,0:T(1,128)}) custom-call(f32[16,16,512]{2,1,0:T(8,128)} %dist_ref.1, f32[8,128]{1,0:T(8,128)} %bitcast.5, bf16[32,2,16,1024]{3,2,1,0:T(8,128)(2,1)} %bitcast.3, bf16[32,2,16,1024]{3,2,1,0:T(8,128)(2,1)} %bitcast.4, f32[16,512]{1,0:T(8,128)} %rate_ref.1), custom_call_target="tpu_custom_call" | custom-call | tf_op jit(solution)/shard_map/boltzmann/pallas_call | solution.py:411
  57.5 2.3 %place.1 = f32[16,16,512]{2,1,0:T(8,128)} custom-call(bf16[64,16,128]{2,1,0:T(8,128)(2,1)} %get-tuple-element.7.tiles_ref, f32[64,1,128]{2,1,0:T(1,128)} %get-tuple-element.8.unit_ref), custom_call_target="tpu_custom_call" | custom-call | tf_op jit(solution)/shard_map/place/pallas_call | solution.py:457

commit v3 on v2

--- a/solution.py
+++ b/solution.py
@@ -25,10 +25,6 @@
     [(dx, dz) for dx in range(RING) for dz in range(RING) if (dx, dz) != (0, 0)],
     key=lambda o: -(min(o[0], RING - o[0]) + min(o[1], RING - o[1])),
 )
-BACK = sorted(
-    [(j, dx) for j in range(4) for dx in range(RING)],
-    key=lambda o: -(min(2 * o[0], RING - 2 * o[0]) + min(o[1], RING - o[1])),
-)
 
 
 def coords():
@@ -68,19 +64,21 @@
     return jnp.where(powers < 0.0, -root, root)
 
 
-def minmod(a, b):
-    return jnp.maximum(jnp.minimum(a, b), 0.0) + jnp.minimum(jnp.maximum(a, b), 0.0)
-
-
-def sweep(values, up, down, ahead, behind):
+def sweep(values, speed, rising, reach):
     n = len(values)
     differ = [values[i + 1] - values[i] for i in range(n - 1)]
-    slopes = [None] + [minmod(differ[i], differ[i - 1]) for i in range(1, n - 1)]
+    slopes = [None] + [
+        jnp.maximum(
+            jnp.minimum(differ[i], jnp.maximum(differ[i - 1], 0.0)),
+            jnp.minimum(differ[i - 1], 0.0),
+        )
+        for i in range(1, n - 1)
+    ]
     fluxes = {}
     for i in range(1, n - 2):
-        fluxes[i] = up * (values[i] + ahead * slopes[i]) + down * (
-            values[i + 1] - behind * slopes[i + 1]
-        )
+        value = jnp.where(rising, values[i], values[i + 1])
+        slope = jnp.where(rising, slopes[i], slopes[i + 1])
+        fluxes[i] = speed * (value + reach * slope)
     return {i: fluxes[i] - fluxes[i - 1] for i in range(2, n - 2)}
 
 
@@ -89,7 +87,7 @@
     sin, send, recv, state, later, smooth, ownr, parr, halo, raw, turned, first, second,
     cour, rates, rate_cols, rate_b, sout, sunit,
     in_sem, mat_sem, a2a_ss, a2a_rs, halo_ss, halo_rs, core_ss, core_rs,
-    rate_sem, out_ss, out_rs, unit_ss, unit_rs,
+    rate_sem, out_ss, out_rs, unit_ss, unit_rs, gone,
 ):
     x, y, z_hi, z_lo, core = coords()
     z = z_hi * 2 + z_lo
@@ -194,6 +192,12 @@
         for i in range(SLAB):
             rate_b[i] = jnp.broadcast_to(column[:, i:i + 1], (PB, LANES))
 
+    sent = send.at[0, pl.ds(0, len(OFFSETS))]
+    pltpu.make_async_copy(sent, sent, a2a_ss.at[0]).wait()
+    pl.semaphore_signal(gone, 1, device_id=twin, device_id_type=MESH)
+    pl.semaphore_wait(gone, 1)
+    send_phase(1)
+
     def arrived(phase):
         pltpu.make_async_copy(recv.at[phase], recv.at[phase], a2a_rs.at[phase]).wait()
 
@@ -224,8 +228,8 @@
         for t in range(4):
             cols = slice(t * LANES, (t + 1) * LANES)
             c = cour[t]
-            up, down = jnp.maximum(c, 0.0), jnp.minimum(c, 0.0)
-            ahead, behind = 0.5 * (1.0 - c), 0.5 * (1.0 + c)
+            rising = c > 0.0
+            reach = jnp.where(rising, 0.5 * (1.0 - c), -(0.5 * (1.0 + c)))
             planes = []
             for i in range(lo - HALO, lo + count + HALO):
                 if i < 0:
@@ -234,9 +238,9 @@
                     planes.append(halo[step, 1, i - SLAB, :, cols])
                 else:
                     planes.append(source[i, :, cols])
-            less = sweep(planes, up, down, ahead, behind)
+            less = sweep(planes, c, rising, reach)
             section = [planes[i] - less[i] for i in range(2, len(planes) - 2)]
-            less2 = sweep(section, up, down, ahead, behind)
+            less2 = sweep(section, c, rising, reach)
             result = [
                 0.5 * planes[i + 2] + 0.5 * (section[i] - less2[i])
                 for i in range(2, len(section) - 2)
@@ -287,7 +291,6 @@
                     )
 
     arrived(0)
-    send_phase(1)
     unpack(0)
     faces = send_faces(state, 0)
     spread_rates()
@@ -320,14 +323,13 @@
     for c in faces:
         c.wait()
 
-    def dispatch(zl):
-        odd = lax.rem(z_lo + zl, 2)
-        for j, dx in BACK:
-            xx, zz = far((dx, 2 * j + odd))
-            t = zz // 2
+    def dispatch(z_to):
+        t, zl = z_to // 2, z_to % 2
+        for dx in (4, 3, 5, 2, 6, 1, 7, 0):
+            xx = lax.rem(x + RING + turn * dx, RING)
 
             def remote():
-                to = device(xx, y, zz, core)
+                to = device(xx, y, z_to, core)
                 pltpu.make_async_remote_copy(
                     sunit.at[zl], unit_ref.at[block], unit_ss, unit_rs,
                     device_id=to, device_id_type=MESH,
@@ -337,12 +339,12 @@
                     device_id=to, device_id_type=MESH,
                 ).start()
 
-            if j or dx:
+            if dx:
                 remote()
             else:
-                pl.when(odd == 1)(remote)
-
-                @pl.when(odd == 0)
+                pl.when(z != z_to)(remote)
+
+                @pl.when(z == z_to)
                 def _():
                     pltpu.make_async_copy(sunit.at[zl], unit_ref.at[block], unit_rs).start()
                     pltpu.make_async_copy(sout.at[zl, x, t], out_ref.at[block], out_rs).start()
@@ -376,7 +378,10 @@
             ]
             for g in range(8):
                 sout[zl, g, t] = jnp.concatenate([pair[0][g], pair[1][g]], axis=0).astype(BF16)
-        dispatch(zl)
+        for z_to in (zl, zl + 2):
+            dispatch(z_to)
+    for z_to in (4, 5, 6, 7):
+        dispatch(z_to)
 
     pltpu.make_async_copy(out_ref, out_ref, out_rs).wait()
     pltpu.make_async_copy(unit_ref, unit_ref, unit_rs).wait()
@@ -384,9 +389,8 @@
     pltpu.make_async_copy(sent, sent, out_ss).wait()
     sent = unit_ref.at[pl.ds(0, len(OFFSETS))]
     pltpu.make_async_copy(sent, sent, unit_ss).wait()
-    for phase in range(2):
-        sent = send.at[0, pl.ds(0, len(OFFSETS))]
-        pltpu.make_async_copy(sent, sent, a2a_ss.at[phase]).wait()
+    sent = send.at[0, pl.ds(0, len(OFFSETS))]
+    pltpu.make_async_copy(sent, sent, a2a_ss.at[1]).wait()
 
 
 def place(tiles_ref, unit_ref, out_ref):
@@ -443,7 +447,7 @@
             pltpu.VMEM((2, 8, 4, 2 * PB, LANES), BF16),
             pltpu.VMEM((2, 1, LANES), F32),
             dma, dma((2,)), dma((2,)), dma((2,)), dma((STEPS, 2)), dma((STEPS, 2)),
-            dma((6,)), dma((6,)), dma((2,)), dma, dma, dma, dma,
+            dma((6,)), dma((6,)), dma((2,)), dma, dma, dma, dma, pltpu.SemaphoreType.REGULAR,
         ],
         compiler_params=pltpu.CompilerParams(collective_id=0, has_side_effects=True),
         name="boltzmann",

time: 60.1 us -> 59.1 us (0.983)
  Pallas kernels: 59.8 us -> 58.6 us
    pallas_call x1, Pallas kernels: 57.5 us -> 56.3 us  [body(): pl.pallas_call(kernel, out_shape=(jax.ShapeDtypeStruct((64, 2 * PB, LANES...]
where the time goes in v3:
time: 59.1 us; the launch traced here: 58.6 us
  Pallas kernels  58.6 us (99%)
    pallas_call x1, Pallas kernels, body(): pl.pallas_call(kernel, out_shape=(jax.ShapeDtypeStruct((64, 2 * PB, LANES...  56.3 us
    pallas_call x1, Pallas kernels, body(): pl.pallas_call(place, out_shape=jax.ShapeDtypeStruct((GROUP, 16, 512), F3...  2.27 us

profile of v3, /device:TPU:1, one launch (start us, length us, event | category | flops | bytes accessed | tf_op | source)
XLA Modules:
  0.0 58.6 jit_solution(13219272170377261346)
XLA Ops:
  0.0 56.3 %boltzmann.1 = (bf16[64,16,128]{2,1,0:T(8,128)(2,1)}, f32[64,1,128]{2,1,0:T(1,128)}) custom-call(f32[16,16,512]{2,1,0:T(8,128)} %dist_ref.1, f32[8,128]{1,0:T(8,128)} %bitcast.5, bf16[32,2,16,1024]{3,2,1,0:T(8,128)(2,1)} %bitcast.3, bf16[32,2,16,1024]{3,2,1,0:T(8,128)(2,1)} %bitcast.4, f32[16,512]{1,0:T(8,128)} %rate_ref.1), custom_call_target="tpu_custom_call" | custom-call | tf_op jit(solution)/shard_map/boltzmann/pallas_call | solution.py:415
  56.3 2.3 %place.1 = f32[16,16,512]{2,1,0:T(8,128)} custom-call(bf16[64,16,128]{2,1,0:T(8,128)(2,1)} %get-tuple-element.7.tiles_ref, f32[64,1,128]{2,1,0:T(1,128)} %get-tuple-element.8.unit_ref), custom_call_target="tpu_custom_call" | custom-call | tf_op jit(solution)/shard_map/place/pallas_call | solution.py:461

commit v4 on v3

--- a/solution.py
+++ b/solution.py
@@ -378,9 +378,8 @@
             ]
             for g in range(8):
                 sout[zl, g, t] = jnp.concatenate([pair[0][g], pair[1][g]], axis=0).astype(BF16)
-        for z_to in (zl, zl + 2):
-            dispatch(z_to)
-    for z_to in (4, 5, 6, 7):
+        dispatch(zl)
+    for z_to in range(2, RING):
         dispatch(z_to)
 
     pltpu.make_async_copy(out_ref, out_ref, out_rs).wait()

time: 59.1 us -> 58.7 us (level)
  no operation moved by 1% of the time
where the time goes in v4:
time: 58.7 us; the launch traced here: 58.5 us
  Pallas kernels  58.5 us (100%)
    pallas_call x1, Pallas kernels, body(): pl.pallas_call(kernel, out_shape=(jax.ShapeDtypeStruct((64, 2 * PB, LANES...  56.2 us
    pallas_call x1, Pallas kernels, body(): pl.pallas_call(place, out_shape=jax.ShapeDtypeStruct((GROUP, 16, 512), F3...  2.28 us

profile of v4, /device:TPU:1, one launch (start us, length us, event | category | flops | bytes accessed | tf_op | source)
XLA Modules:
  0.0 58.5 jit_solution(15677440775267567346)
XLA Ops:
  0.0 56.2 %boltzmann.1 = (bf16[64,16,128]{2,1,0:T(8,128)(2,1)}, f32[64,1,128]{2,1,0:T(1,128)}) custom-call(f32[16,16,512]{2,1,0:T(8,128)} %dist_ref.1, f32[8,128]{1,0:T(8,128)} %bitcast.5, bf16[32,2,16,1024]{3,2,1,0:T(8,128)(2,1)} %bitcast.3, bf16[32,2,16,1024]{3,2,1,0:T(8,128)(2,1)} %bitcast.4, f32[16,512]{1,0:T(8,128)} %rate_ref.1), custom_call_target="tpu_custom_call" | custom-call | tf_op jit(solution)/shard_map/boltzmann/pallas_call | solution.py:414
  56.2 2.3 %place.1 = f32[16,16,512]{2,1,0:T(8,128)} custom-call(bf16[64,16,128]{2,1,0:T(8,128)(2,1)} %get-tuple-element.7.tiles_ref, f32[64,1,128]{2,1,0:T(1,128)} %get-tuple-element.8.unit_ref), custom_call_target="tpu_custom_call" | custom-call | tf_op jit(solution)/shard_map/place/pallas_call | solution.py:460
